TPU v7x, 32 devices: a whole 2x2x4 slice. The times are simulated.
32 devices in a mesh: stretch: 8 (over y, x, core), fsdp: 4 (over z).
Axes of the slice: x: 2, y: 2, z: 4, core: 2. Of those that a mesh axis runs over, the one named last changes fastest.
Arguments:
- latents: bfloat16 [8, 3, 192, 6144], P('stretch', None, 'fsdp'), may hold values from -6 to 6
- step_index: int32 [8, 3], P('stretch'), may hold values from 0 to 49
- block_mask: int32 [8, 8], replicated, may hold values from 0 to 1, as said below
- mod_table: bfloat16 [50, 2, 6144], replicated, may hold values from -2 to 2
- w_query: bfloat16 [6144, 4096], P(None, 'fsdp')
- w_key: bfloat16 [6144, 4096], P(None, 'fsdp')
- w_value: bfloat16 [6144, 4096], P(None, 'fsdp'), may hold values from -0.078125 to 0.078125
Outputs:
- attended: bfloat16 [8, 3, 192, 4096], P('stretch', None, None, 'fsdp')
Inputs may be any that keep to these rules, and one draw needn't show every extreme that they name: block_mask[c, c] and block_mask[c, 0] are 1 and block_mask[c, c2] is 0 for c2 > c; other entries below the diagonal are 0 or 1.
All inputs are finite; a program needn't handle non-finite values.
Results may differ from a plain program's by a relative error of at most 0.011.
Values may be sent and summed in bfloat16 or wider, within the bound.
No kernel may reach another device: no remote copies, remote signals or barrier semaphores. Data moves between devices by JAX's collectives and lax.ppermute only.
A program may use at most 192 MiB of HBM per device.

v0:
```python
import jax
import jax.numpy as jnp
from jax import lax
from jax.sharding import PartitionSpec as P

HEAD_DIM = 128


def modulate(latents, step_index, mod_table):
    width = latents.shape[-1]
    levels = mod_table.shape[0]
    values = latents.astype(jnp.float32)
    normed = values * lax.rsqrt(jnp.mean(values * values, axis=-1, keepdims=True) + 1e-06)
    onehot = (step_index[..., None] == jnp.arange(levels, dtype=jnp.int32)).astype(jnp.bfloat16)
    mods = jnp.einsum(
        "cbs,sd->cbd",
        onehot,
        mod_table.reshape(levels, 2 * width),
        preferred_element_type=jnp.float32,
    )
    scale = mods[..., :width][:, :, None, :]
    shift = mods[..., width:][:, :, None, :]
    return (normed * (1.0 + scale) + shift).astype(jnp.bfloat16)


def attend_piece(carry, pieces, block_ids, queries, mask_row):
    run_max, total, summed = carry
    keys, values = pieces
    count, videos, tokens = (keys.shape[0], keys.shape[1], keys.shape[2])
    keys = keys.reshape(count, videos, tokens, -1, HEAD_DIM)
    values = values.reshape(count, videos, tokens, -1, HEAD_DIM)
    known = jnp.arange(mask_row.shape[0], dtype=jnp.int32)[None, :] == block_ids[:, None]
    allowed = jnp.sum(jnp.where(known, mask_row[None, :], 0), axis=1) > 0
    allowed = allowed[None, None, None, :, None]
    scores = jnp.einsum("bqhd,nbkhd->bhqnk", queries, keys, preferred_element_type=jnp.float32)
    scores = scores * (1.0 / jnp.sqrt(jnp.float32(HEAD_DIM)))
    masked = jnp.where(allowed, scores, jnp.float32(-1e30))
    new_max = jnp.maximum(run_max, jnp.max(masked, axis=(3, 4)))
    weights = jnp.where(allowed, jnp.exp(masked - new_max[..., None, None]), jnp.float32(0.0))
    total = jnp.sum(weights, axis=(3, 4))
    rounded = weights.astype(jnp.bfloat16)
    update = jnp.einsum("bhqnk,nbkhd->bhqd", rounded, values, preferred_element_type=jnp.float32)
    summed = update
    return (new_max, total, summed)


def shards(latents, step_index, block_mask, mod_table, w_query, w_key, w_value):
    modulated = modulate(latents, step_index, mod_table)
    width = modulated.shape[-1]
    local_cols = w_query.shape[1]
    w_joined = jnp.concatenate([w_query, w_key, w_value], axis=1)
    piece = lax.all_gather(modulated, "fsdp", axis=2, tiled=True)
    flat = piece.reshape(-1, width)
    result = jnp.dot(flat, w_joined, preferred_element_type=jnp.float32).astype(jnp.bfloat16)
    projected = result.reshape(piece.shape[0], piece.shape[1], piece.shape[2], 3 * local_cols)
    queries = projected[..., :local_cols]
    keys = projected[..., local_cols : 2 * local_cols]
    values = projected[..., 2 * local_cols :]
    videos, tokens = (queries.shape[1], queries.shape[2])
    local_heads = local_cols // HEAD_DIM
    query_rows = queries[0]
    queries = query_rows.reshape(videos, tokens, local_heads, HEAD_DIM)
    own_group = lax.axis_index("stretch")
    mask_row = lax.dynamic_slice_in_dim(block_mask, own_group, 1, 0)[0]
    start_carry = (
        jnp.full((videos, local_heads, tokens), -1e30, jnp.float32),
        jnp.zeros((videos, local_heads, tokens), jnp.float32),
        jnp.zeros((videos, local_heads, tokens, HEAD_DIM), jnp.float32),
    )
    pieces = (
        lax.all_gather(keys, "stretch", axis=0, tiled=True),
        lax.all_gather(values, "stretch", axis=0, tiled=True),
    )
    block_ids = jnp.arange(pieces[0].shape[0], dtype=jnp.int32)
    final = attend_piece(start_carry, pieces, block_ids, queries, mask_row)
    run_max, total, summed = final
    result = summed / total[..., None]
    result = jnp.transpose(result, (0, 2, 1, 3)).reshape(1, videos, tokens, local_cols)
    return result.astype(jnp.bfloat16)


def solution(mesh):
    placed = (
        P("stretch", None, "fsdp", None),
        P("stretch", None),
        P(),
        P(),
        P(None, "fsdp"),
        P(None, "fsdp"),
        P(None, "fsdp"),
    )
    return jax.shard_map(
        shards,
        mesh=mesh,
        in_specs=placed,
        out_specs=P("stretch", None, None, "fsdp"),
        check_vma=False,
    )
```

profile of v0, /device:TPU:0, one launch (start us, length us, event | category | flops | bytes accessed | tf_op | source)
XLA Modules:
  0.0 345.2 jit_solution(2279670905428013449)
XLA Ops:
  6.5 0.0 copy-start
  6.5 0.0 copy-start.2
  6.5 0.0 all-gather.4.cloned.1.call-start
  6.5 2.4 pad.3
  9.0 0.4 copy.29
  9.4 1.0 convolution_bitcast_fusion
  10.5 1.9 fusion.18
  12.4 0.0 copy-done.2
  12.4 1.9 fusion.21
  14.3 0.0 all-gather.4.cloned.1.call-update
  14.3 0.0 all-gather.6.cloned.1.call-start
  14.4 131.0 %all-gather.4.cloned.1.call-done = bf16[1,3,192,6144]{3,2,1,0:T(8,128)(2,1)} async-done(((bf16[1,3,48,6144]{3,2,1,0:T(8,128)(2,1)}), bf16[1,3,192,6144]{3,2,1,0:T(8,128)(2,1)}) %all-gather.4.cloned.1.call-update) | async-done | bytes 7077904 | tf_op jit(solution)/shard_map/all_gather | solution.py:52
  145.4 26.7 %fusion.15 = bf16[576,3072]{1,0:T(8,128)(2,1)S(1)} fusion(bf16[576,6144]{1,0:T(8,128)(2,1)} %bitcast.59, bf16[6144,1024]{1,0:T(8,128)(2,1)} %param.13, bf16[6144,1024]{1,0:T(8,128)(2,1)} %param.12, bf16[6144,1024]{1,0:T(8,128)(2,1)} %param.11), kind=kOutput, calls=%fused_computation.17 | convolution fusion | flops 21858287616 | bytes 48365568 | tf_op jit(solution)/shard_map/dot_general | solution.py:54
  172.1 1.7 fusion.36
  173.8 0.0 all-gather.6.cloned.1.call-update
  173.8 0.0 all-gather.8.cloned.1.call-start
  173.9 0.7 all-gather.8.cloned.1.call-update
  174.6 0.0 copy-done
  174.6 0.1 select_reduce_fusion
  174.7 0.3 copy.30
  175.0 0.1 bitcast_bitcast_fusion
  175.1 55.7 %all-gather.6.cloned.1.call-done = bf16[8,3,192,1024]{3,2,1,0:T(8,128)(2,1)} async-done(((bf16[1,3,192,1024]{3,2,1,0:T(8,128)(2,1)}), bf16[8,3,192,1024]{3,2,1,0:T(8,128)(2,1)}) %all-gather.6.cloned.1.call-update) | async-done | bytes 9437200 | tf_op jit(solution)/shard_map/all_gather | solution.py:71
  230.9 10.0 %copy.31 = bf16[576,8,8,128]{3,2,1,0:T(8,128)(2,1)} copy(bf16[576,8,8,128]{3,1,2,0:T(8,128)(2,1)} %bitcast.49) | data formatting | bytes 18874368
  240.9 18.0 %fusion.6 = (f32[3,8,192]{2,1,0:T(8,128)S(1)}, f32[3,8,192,8,192]{2,4,3,1,0:T(8,128)}) fusion(pred[8]{0:T(512)(128)(4,1)S(1)} %broadcast_compare_fusion, bf16[8,3,192,8,128]{4,3,2,1,0:T(8,128)(2,1)} %bitcast.51, bf16[3,192,8,128,1]{3,2,1,0,4:T(8,128)(2,1)S(1)} %bitcast_bitcast_fusion), kind=kOutput, calls=%fused_computation.8 | convolution fusion | flops 1833168384 | bytes 38946824 | tf_op jit(solution)/shard_map/bqhd,nbkhd->bhqnk/dot_general | solution.py:35
  258.9 32.5 %all-gather.8.cloned.1.call-done = bf16[8,3,192,1024]{3,2,1,0:T(8,128)(2,1)} async-done(((bf16[1,3,192,1024]{3,2,1,0:T(8,128)(2,1)}), bf16[8,3,192,1024]{3,2,1,0:T(8,128)(2,1)}) %all-gather.8.cloned.1.call-update) | async-done | bytes 9437200 | tf_op jit(solution)/shard_map/all_gather | solution.py:72
  291.5 9.6 %copy.32 = bf16[576,8,8,128]{3,2,1,0:T(8,128)(2,1)} copy(bf16[576,8,8,128]{3,1,2,0:T(8,128)(2,1)} %bitcast.48) | data formatting | bytes 18874368
  301.1 16.9 %fusion.7 = f32[3,8,192]{2,1,0:T(8,128)S(1)} fusion(f32[3,8,192,8,192]{2,4,3,1,0:T(8,128)} %get-tuple-element.11, f32[3,8,192]{2,1,0:T(8,128)S(1)} %broadcast_maximum_fusion, pred[8]{0:T(512)(128)(4,1)S(1)} %broadcast_compare_fusion), kind=kLoop, calls=%fused_computation.9 | loop fusion | flops 35384832 | bytes 28348424 | tf_op jit(solution)/shard_map/reduce_sum | solution.py:40
  318.0 0.0 copy-start.1
  318.1 18.5 %fusion.22 = bf16[3,192,8,128]{3,1,2,0:T(8,128)(2,1)S(1)} fusion(bf16[8,3,192,8,128]{4,3,2,1,0:T(8,128)(2,1)} %bitcast.50, f32[3,8,192,8,192]{2,4,3,1,0:T(8,128)} %get-tuple-element.11, f32[3,8,192]{2,1,0:T(8,128)S(1)} %broadcast_maximum_fusion, pred[8]{0:T(512)(128)(4,1)S(1)} %broadcast_compare_fusion, f32[3,192,8]{1,2,0:T(8,128)S(1)} %bitcast.57), kind=kOutput, calls=%fused_computation.25 | convolution fusion | flops 1848508416 | bytes 38965256 | tf_op jit(solution)/shard_map/bhqnk,nbkhd->bhqd/dot_general | solution.py:42
  336.6 0.8 copy.23
  337.3 1.4 convert_element_type.32
  338.7 0.0 copy-done.1
  (5 shorter events, 0.1 us)
Async XLA Ops:
  6.5 168.0 %copy-start = (s32[8,8]{1,0:T(8,128)S(1)}, s32[8,8]{1,0:T(8,128)}, u32[]{:S(2)}) copy-start(s32[8,8]{1,0:T(8,128)} %param.9) | copy-start | bytes 772
  6.5 5.9 %copy-start.2 = (bf16[1,3,48,6144]{3,2,1,0:T(8,128)(2,1)S(1)}, bf16[1,3,48,6144]{3,2,1,0:T(8,128)(2,1)}, u32[]{:S(2)}) copy-start(bf16[1,3,48,6144]{3,2,1,0:T(8,128)(2,1)} %param.7) | copy-start | bytes 5308420
  6.5 138.9 %all-gather.4.cloned.1.call-start = ((), (), s32[]{:S(2)}) async-start(), calls=%async_computation | async-start | bytes 8847360 | tf_op jit(solution)/shard_map/all_gather | solution.py:52
  14.3 216.5 %all-gather.6.cloned.1.call-start = ((), (), s32[]{:S(2)}) async-start(), calls=%async_computation.1 | async-start | bytes 10616832 | tf_op jit(solution)/shard_map/all_gather | solution.py:71
  173.8 117.7 %all-gather.8.cloned.1.call-start = ((), (), s32[]{:S(2)}) async-start(), calls=%async_computation.2 | async-start | bytes 10616832 | tf_op jit(solution)/shard_map/all_gather | solution.py:72
  318.0 20.7 %copy-start.1 = (s32[8,8]{1,0:T(8,128)S(1)}, s32[8,8]{1,0:T(8,128)}, u32[]{:S(2)}) copy-start(s32[8,8]{1,0:T(8,128)} %param.9) | copy-start | bytes 772
Sparse Core Ops, SparseCore 0:
  14.4 130.8 all-gather.3
  173.9 56.8 all-gather.5
  232.7 58.6 all-gather.7
where the time goes:
time: 346 us; the launch traced here: 345 us
  waiting for transfers between devices  220 us (64%)
  matrix products  64.2 us (19%)
  local copies, waits for them, and re-layouts  26.8 us (8%)
  other arithmetic  20.9 us (6%)
  between operations  13.2 us (4%)
    all_gather x1, waiting for transfers between devices, shards(): piece = lax.all_gather(modulated, 'fsdp', axis=2, tiled=True)  131 us
    all_gather x1, waiting for transfers between devices, shards(): lax.all_gather(keys, 'stretch', axis=0, tiled=True)  55.7 us
    all_gather x1, waiting for transfers between devices, shards(): lax.all_gather(values, 'stretch', axis=0, tiled=True)  32.5 us
    dot_general x1, matrix products, shards(): jnp.dot(flat, w_joined, preferred_element_type=jnp.float32)  26.7 us
    unnamed x11, local copies, waits for them, and re-layouts  22.9 us
    dot_general x1, matrix products, attend_piece(): jnp.einsum('bhqnk,nbkhd->bhqd', rounded, values, preferred_element_type=j...  18.5 us
    dot_general x1, matrix products, attend_piece(): jnp.einsum('bqhd,nbkhd->bhqnk', queries, keys, preferred_element_type=jnp...  18 us
    reduce_sum x1, other arithmetic, attend_piece(): total = jnp.sum(weights, axis=(3, 4))  16.9 us
  transfers between devices with their start and end apart: 3, of which 3 were waited for; matrix products, arithmetic and copies ran while one was open for 8% of the time, Pallas kernels for 0%

commit v1 on v0

v1 whole, which is shorter than its diff:
```python
import functools

import jax
import jax.numpy as jnp
from jax import lax
from jax.experimental import pallas as pl
from jax.experimental.pallas import tpu as pltpu
from jax.sharding import PartitionSpec as P


HEAD_DIM = 128
LOG2E = 1.4426950408889634


def modulate(latents, step_index, mod_table):
    width = latents.shape[-1]
    levels = mod_table.shape[0]
    values = latents.astype(jnp.float32)
    normed = values * lax.rsqrt(jnp.mean(values * values, axis=-1, keepdims=True) + 1e-06)
    onehot = (step_index[..., None] == jnp.arange(levels, dtype=jnp.int32)).astype(jnp.bfloat16)
    mods = jnp.einsum(
        "cbs,sd->cbd",
        onehot,
        mod_table.reshape(levels, 2 * width),
        preferred_element_type=jnp.float32,
    )
    scale = mods[..., :width][:, :, None, :]
    shift = mods[..., width:][:, :, None, :]
    return (normed * (1.0 + scale) + shift).astype(jnp.bfloat16)


def plain_shards(latents, step_index, block_mask, mod_table, w_query, w_key, w_value):
    modulated = modulate(latents, step_index, mod_table)
    width = modulated.shape[-1]
    local_cols = w_query.shape[1]
    w_joined = jnp.concatenate([w_query, w_key, w_value], axis=1)
    piece = lax.all_gather(modulated, "fsdp", axis=2, tiled=True)
    flat = piece.reshape(-1, width)
    result = jnp.dot(flat, w_joined, preferred_element_type=jnp.float32).astype(jnp.bfloat16)
    projected = result.reshape(piece.shape[0], piece.shape[1], piece.shape[2], 3 * local_cols)
    videos, tokens = projected.shape[1:3]
    heads = local_cols // HEAD_DIM
    queries = projected[0, ..., :local_cols].reshape(videos, tokens, heads, HEAD_DIM)
    keys = lax.all_gather(projected[..., local_cols : 2 * local_cols], "stretch", axis=0, tiled=True)
    values = lax.all_gather(projected[..., 2 * local_cols :], "stretch", axis=0, tiled=True)
    keys = keys.reshape(-1, videos, tokens, heads, HEAD_DIM)
    values = values.reshape(-1, videos, tokens, heads, HEAD_DIM)
    mask_row = lax.dynamic_slice_in_dim(block_mask, lax.axis_index("stretch"), 1, 0)[0]
    allowed = (mask_row > 0)[None, None, None, :, None]
    scores = jnp.einsum("bqhd,nbkhd->bhqnk", queries, keys, preferred_element_type=jnp.float32)
    scores = scores * (1.0 / jnp.sqrt(jnp.float32(HEAD_DIM)))
    masked = jnp.where(allowed, scores, jnp.float32(-1e30))
    row_max = jnp.max(masked, axis=(3, 4), keepdims=True)
    weights = jnp.where(allowed, jnp.exp(masked - row_max), jnp.float32(0.0))
    total = jnp.sum(weights, axis=(3, 4))
    summed = jnp.einsum(
        "bhqnk,nbkhd->bhqd", weights.astype(jnp.bfloat16), values, preferred_element_type=jnp.float32
    )
    result = jnp.transpose(summed / total[..., None], (0, 2, 1, 3))
    return result.reshape(1, videos, tokens, local_cols).astype(jnp.bfloat16)


def hold_kernel(*refs):
    *refs, sems = refs
    count = len(refs) // 2
    copies = []
    for index, (source, target) in enumerate(zip(refs[:count], refs[count:])):
        for group in range(target.shape[0]):
            columns = slice(group * target.shape[2], (group + 1) * target.shape[2])
            copies.append(pltpu.make_async_copy(source.at[:, columns], target.at[group], sems.at[index, group]))
    for copy in copies:
        copy.start()
    for copy in copies:
        copy.wait()


def hold(*arrays):
    width, columns = arrays[0].shape
    wide = 2 * HEAD_DIM
    groups = columns // wide
    arrays = [pltpu.with_memory_space_constraint(array, pltpu.HBM) for array in arrays]
    return pl.pallas_call(
        hold_kernel,
        out_shape=[pltpu.VMEM((groups, width, wide), array.dtype) for array in arrays],
        in_specs=[pl.BlockSpec(memory_space=pltpu.HBM)] * len(arrays),
        out_specs=[pl.BlockSpec(memory_space=pltpu.VMEM)] * len(arrays),
        scratch_shapes=[pltpu.SemaphoreType.DMA((len(arrays), groups))],
        compiler_params=pltpu.CompilerParams(vmem_limit_bytes=1 << 20),
        cost_estimate=pl.CostEstimate(
            flops=0, bytes_accessed=len(arrays) * width * columns * 2, transcendentals=0
        ),
    )(*arrays)


def modulate_kernel(steps_ref, own_ref, below_ref, above_ref, far_ref, farthest_ref, mod_ref, x_ref):
    place = lax.axis_index("fsdp")
    ranks = 4
    share = own_ref.shape[0]
    rows = 16
    gain = 1.0 + mod_ref[0, 0:1, :].astype(jnp.float32)
    shift = mod_ref[0, 1:2, :].astype(jnp.float32)

    def fill(piece, slot):
        @pl.loop(0, share // rows)
        def _(row):
            inside = pl.multiple_of(row * rows, rows)
            values = piece[pl.ds(inside, rows), :].astype(jnp.float32)
            mean = jnp.mean(values * values, axis=-1, keepdims=True)
            normed = values * lax.rsqrt(mean + 1e-06)
            start = pl.multiple_of(slot * share + inside, rows)
            x_ref[pl.ds(start, rows), :] = (normed * gain + shift).astype(jnp.bfloat16)

    fill(own_ref, place)
    fill(far_ref, lax.rem(place + 2, ranks))
    pl.when(place >= 1)(lambda: fill(below_ref, place - 1))
    pl.when(place <= ranks - 2)(lambda: fill(above_ref, place + 1))
    pl.when((place == 0) | (place == ranks - 1))(lambda: fill(farthest_ref, ranks - 1 - place))


def modulate_pieces(video, steps, pieces, mod_table):
    share, width = pieces[0].shape
    tokens = share * 4
    whole = pl.BlockSpec(memory_space=pltpu.VMEM)
    return pl.pallas_call(
        modulate_kernel,
        out_shape=pltpu.VMEM((tokens, width), jnp.bfloat16),
        grid_spec=pltpu.PrefetchScalarGridSpec(
            num_scalar_prefetch=1,
            grid=(1,),
            in_specs=[whole] * len(pieces)
            + [pl.BlockSpec((1, 2, width), lambda j, steps: (steps[video], 0, 0), pipeline_mode=pl.Buffered(1))],
            out_specs=whole,
        ),
        compiler_params=pltpu.CompilerParams(vmem_limit_bytes=10 << 20),
        cost_estimate=pl.CostEstimate(flops=10 * tokens * width, bytes_accessed=4 * tokens * width, transcendentals=0),
    )(steps, *pieces, mod_table)


def project_kernel(pairs, x_ref, wq_ref, wk_ref, wv_ref, *out_refs):
    own = lax.axis_index("stretch")
    odd = lax.rem(own, 2)
    for index, pair in enumerate(pairs):
        for part, w_ref in enumerate((wq_ref, wk_ref, wv_ref)):
            result = jnp.dot(x_ref[...], w_ref[own // 2 ^ pair], preferred_element_type=jnp.float32)
            result = result.astype(jnp.bfloat16)
            low, high = result[:, :HEAD_DIM], result[:, HEAD_DIM:]
            place = slice(part * HEAD_DIM, (part + 1) * HEAD_DIM)
            out_refs[2 * index][:, place] = jnp.where(odd == 0, low, high)
            out_refs[2 * index + 1][:, place] = jnp.where(odd == 0, high, low)


def project(pairs, x, weights):
    tokens, width = x.shape
    whole = pl.BlockSpec(memory_space=pltpu.VMEM)
    columns = 6 * HEAD_DIM * len(pairs)
    return pl.pallas_call(
        functools.partial(project_kernel, pairs),
        out_shape=[jax.ShapeDtypeStruct((tokens, 3 * HEAD_DIM), jnp.bfloat16)] * (2 * len(pairs)),
        in_specs=[whole] * (1 + len(weights)),
        out_specs=[whole] * (2 * len(pairs)),
        compiler_params=pltpu.CompilerParams(vmem_limit_bytes=8 << 20),
        cost_estimate=pl.CostEstimate(
            flops=2 * tokens * width * columns, bytes_accessed=2 * tokens * columns, transcendentals=0
        ),
    )(x, *weights)


def attend_kernel(mask_ref, *refs):
    groups = (len(refs) - 2) // 2
    in_refs, out_refs = refs[:groups], refs[groups : 2 * groups]
    qkv_ref, sum_ref = refs[2 * groups :]
    tokens = qkv_ref.shape[1]
    own = lax.axis_index("stretch")
    for index, ref in enumerate(in_refs):
        qkv_ref[own ^ index] = ref[...]
    factor = LOG2E / HEAD_DIM**0.5
    column = lax.broadcasted_iota(jnp.int32, (1, groups * tokens), 1) // tokens
    for seg in range(groups):
        span = (seg + 1) * tokens
        bias = jnp.zeros((1, span), jnp.float32)
        for other in range(seg + 1):
            hidden = jnp.where(mask_ref[seg, other] == 1, 0.0, -1e30).astype(jnp.float32)
            bias = jnp.where(column[:, :span] == other, hidden, bias)
        query = qkv_ref[seg, :, 0:HEAD_DIM]
        keys = qkv_ref[0 : seg + 1, :, HEAD_DIM : 2 * HEAD_DIM].reshape(span, HEAD_DIM)
        values = qkv_ref[0 : seg + 1, :, 2 * HEAD_DIM : 3 * HEAD_DIM].reshape(span, HEAD_DIM)
        scores = lax.dot_general(query, keys, (((1,), (1,)), ((), ())), preferred_element_type=jnp.float32)
        scores = scores * factor + bias
        row_max = jnp.max(scores, axis=-1, keepdims=True)
        weights = jnp.exp2(scores - row_max)
        total = jnp.sum(weights, axis=-1, keepdims=True)
        summed = jnp.dot(weights.astype(jnp.bfloat16), values, preferred_element_type=jnp.float32)
        sum_ref[seg] = (summed / total).astype(jnp.bfloat16)
    for index, ref in enumerate(out_refs):
        ref[...] = sum_ref[own ^ index]


def attend(block_mask, slots):
    groups = len(slots)
    tokens, width = slots[0].shape
    pairs = groups * (groups + 1) // 2 * tokens * tokens
    whole = pl.BlockSpec(memory_space=pltpu.VMEM)
    return pl.pallas_call(
        attend_kernel,
        out_shape=[jax.ShapeDtypeStruct((tokens, HEAD_DIM), jnp.bfloat16)] * groups,
        in_specs=[pl.BlockSpec(memory_space=pltpu.SMEM)] + [whole] * groups,
        out_specs=[whole] * groups,
        scratch_shapes=[
            pltpu.VMEM((groups, tokens, width), jnp.bfloat16),
            pltpu.VMEM((groups, tokens, HEAD_DIM), jnp.bfloat16),
        ],
        compiler_params=pltpu.CompilerParams(vmem_limit_bytes=14 << 20),
        cost_estimate=pl.CostEstimate(
            flops=4 * pairs * HEAD_DIM, bytes_accessed=4 * groups * tokens * HEAD_DIM * 2, transcendentals=pairs
        ),
    )(block_mask, *slots)


def finish_kernel(*refs):
    groups = len(refs) - 1
    out_ref = refs[-1]
    own = lax.axis_index("stretch")
    for index, ref in enumerate(refs[:groups]):
        start = pl.multiple_of((own ^ index) * HEAD_DIM, HEAD_DIM)
        out_ref[0, 0, :, pl.ds(start, HEAD_DIM)] = ref[...]


def finish(video, videos, slots, joined):
    tokens = slots[0].shape[0]
    groups = len(slots)
    whole = pl.BlockSpec(memory_space=pltpu.VMEM)
    shape = (1, 1, tokens, groups * HEAD_DIM)
    extra = () if joined is None else (joined,)

    def body(*refs):
        finish_kernel(*refs[:groups], refs[-1])

    return pl.pallas_call(
        body,
        out_shape=jax.ShapeDtypeStruct((1, videos) + shape[2:], jnp.bfloat16),
        grid=(1,),
        in_specs=[whole] * groups + [pl.BlockSpec(memory_space=pl.ANY)] * len(extra),
        out_specs=pl.BlockSpec(shape, lambda j: (0, video, 0, 0)),
        input_output_aliases={groups: 0} if extra else {},
        compiler_params=pltpu.CompilerParams(vmem_limit_bytes=4 << 20),
    )(*slots, *extra)


SENDS = (6, 7, 2, 3, 4, 5, 1)


def exchange(slots):
    n = len(slots)
    moved = dict(enumerate(slots))
    for index in SENDS:
        moved[index] = lax.ppermute(slots[index], "stretch", [(i, i ^ index) for i in range(n)])
    return [moved[index] for index in range(n)]


def shards(latents, step_index, block_mask, mod_table, w_query, w_key, w_value):
    _, videos, _, _ = latents.shape
    near_up = [(i, i + 1) for i in range(3)]
    near_down = [(i + 1, i) for i in range(3)]
    across = [(0, 2), (1, 3), (2, 0), (3, 1)]
    onward = [(2, 3), (1, 0)]
    steps = step_index[0]
    weights = hold(w_query, w_key, w_value)
    moved = []
    for video in range(videos):
        own = latents[0, video]
        far = lax.ppermute(own, "fsdp", across)
        up = lax.ppermute(own, "fsdp", near_up)
        down = lax.ppermute(own, "fsdp", near_down)
        farthest = lax.ppermute(far, "fsdp", onward)
        moved.append((own, up, down, far, farthest))
    joined = None
    for video, pieces in enumerate(moved):
        x = modulate_pieces(video, steps, pieces, mod_table)
        slots = {}
        order = ((3,), (1, 2), (0,)) if video == videos - 1 else ((3, 1, 2, 0),)
        for part in order:
            made = project(part, x, weights)
            for index, pair in enumerate(part):
                slots[2 * pair], slots[2 * pair + 1] = made[2 * index : 2 * index + 2]
        slots = exchange([slots[index] for index in range(len(slots))])
        slots = attend(block_mask, slots)
        slots = exchange(slots)
        joined = finish(video, videos, slots, joined)
    return joined


def solution(mesh):
    placed = (
        P("stretch", None, "fsdp", None),
        P("stretch", None),
        P(),
        P(),
        P(None, "fsdp"),
        P(None, "fsdp"),
        P(None, "fsdp"),
    )

    def mapped(body):
        return jax.shard_map(
            body, mesh=mesh, in_specs=placed, out_specs=P("stretch", None, None, "fsdp"), check_vma=False
        )

    def run(*args):
        latents, w_query = args[0], args[4]
        parts = mesh.shape["stretch"], mesh.shape["fsdp"]
        share = latents.shape[2] // parts[1]
        heads = w_query.shape[1] // parts[1] // HEAD_DIM
        if parts[1] == 4 and heads == parts[0] == 8 and share % 16 == 0:
            return mapped(shards)(*args)
        return mapped(plain_shards)(*args)

    return run
```

time: 346 us -> 244 us (0.71)
  waiting for transfers between devices: 220 us -> 49.9 us
  starting transfers between devices: 0.09 us -> 89.5 us
  Pallas kernels: 0 us -> 64.8 us
  matrix products: 64.2 us -> 0 us
  other arithmetic: 20.9 us -> 0.01 us
  between operations: 13.2 us -> 0.42 us
  local copies, waits for them, and re-layouts: 26.8 us -> 37.3 us
    all_gather x3 -> x0, waiting for transfers between devices: 219 us -> none  [the longest x1 131 us: shards(): piece = lax.all_gather(modulated, 'fsdp', axis=2, tiled=True)]
    ppermute x0 -> x54, starting transfers between devices: none -> 89.5 us  [the longest x42 40.9 us: exchange(): lax.ppermute(slots[index], 'stretch', [(i, i ^ index) for i in range(n)])]
    pallas_call x0 -> x15, Pallas kernels: none -> 64.8 us  [the longest x5 23.9 us: project(): pl.pallas_call(functools.partial(project_kernel, pairs), out_shape=[jax.S...]
    dot_general x4 -> x0, matrix products: 64.2 us -> none  [the longest x1 26.7 us: shards(): jnp.dot(flat, w_joined, preferred_element_type=jnp.float32)]
    ppermute x0 -> x54, waiting for transfers between devices: none -> 49.9 us  [the longest x3 43.1 us: shards(): far = lax.ppermute(own, 'fsdp', across)]
    reduce_sum x3 -> x0, other arithmetic: 19 us -> none  [the longest x1 16.9 us: attend_piece(): total = jnp.sum(weights, axis=(3, 4))]
    unnamed x11 -> x58, local copies, waits for them, and re-layouts: 22.9 us -> 35.7 us
  transfers between devices with their start and end apart: 3 -> 54, of which waited for: 3 -> 9; matrix products, arithmetic and copies ran while one was open for 8% -> 0% of each run, Pallas kernels for 0% -> 26%
where the time goes in v1:
time: 244 us; the launch traced here: 242 us
  starting transfers between devices  89.5 us (37%)
  Pallas kernels  64.8 us (27%)
  waiting for transfers between devices  49.9 us (20%)
  local copies, waits for them, and re-layouts  37.3 us (15%)
    ppermute x3, waiting for transfers between devices, shards(): far = lax.ppermute(own, 'fsdp', across)  43.1 us
    ppermute x42, starting transfers between devices, exchange(): lax.ppermute(slots[index], 'stretch', [(i, i ^ index) for i in range(n)])  40.9 us
    unnamed x58, local copies, waits for them, and re-layouts  35.7 us
    ppermute x3, starting transfers between devices, shards(): far = lax.ppermute(own, 'fsdp', across)  26.6 us
    pallas_call x5, Pallas kernels, project(): pl.pallas_call(functools.partial(project_kernel, pairs), out_shape=[jax.S...  23.9 us
    ppermute x3, starting transfers between devices, shards(): up = lax.ppermute(own, 'fsdp', near_up)  14.3 us
    pallas_call x3, Pallas kernels, attend(): pl.pallas_call(attend_kernel, out_shape=[jax.ShapeDtypeStruct((tokens, HE...  13.4 us
    pallas_call x3, Pallas kernels, modulate_pieces(): pl.pallas_call(modulate_kernel, out_shape=pltpu.VMEM((tokens, width), jnp...  12.9 us
  transfers between devices with their start and end apart: 54, of which 9 were waited for; matrix products, arithmetic and copies ran while one was open for 0% of the time, Pallas kernels for 26%

profile of v1, /device:TPU:0, one launch (start us, length us, event | category | flops | bytes accessed | tf_op | source)
XLA Modules:
  0.0 241.9 jit_solution(5332590333191489732)
XLA Ops:
  0.0 1.6 slice_bitcast_fusion
  1.6 4.1 %collective-permute-start.2 = (bf16[48,6144]{1,0:T(8,128)(2,1)S(1)}, bf16[48,6144]{1,0:T(8,128)(2,1)S(1)}, u32[]{:S(2)}, u32[]{:S(2)}) collective-permute-start(bf16[48,6144]{1,0:T(8,128)(2,1)S(1)} %get-tuple-element.108.own_ref), channel_id=1, source_target_pairs={{0,2},{1,3},{2,0},{3,1},{4,6},{5,7},{6,4},{7,5},{8,10},{9,11},{10,... | collective-permute-start | bytes 1769480 | tf_op jit(solution)/shard_map/ppermute | solution.py:271
  5.7 3.5 %collective-permute-start = (bf16[48,6144]{1,0:T(8,128)(2,1)S(1)}, bf16[48,6144]{1,0:T(8,128)(2,1)S(1)}, u32[]{:S(2)}, u32[]{:S(2)}) collective-permute-start(bf16[48,6144]{1,0:T(8,128)(2,1)S(1)} %get-tuple-element.108.own_ref), channel_id=1, source_target_pairs={{0,1},{1,2},{2,3},{4,5},{5,6},{6,7},{8,9},{9,10},{10,11},{12,13},{... | collective-permute-start | bytes 1769480 | tf_op jit(solution)/shard_map/ppermute | solution.py:272
  9.2 1.3 collective-permute-start.1
  10.5 2.1 collective-permute-start.20
  12.6 20.8 %collective-permute-done.2.far_ref = bf16[48,6144]{1,0:T(8,128)(2,1)S(1)} collective-permute-done((bf16[48,6144]{1,0:T(8,128)(2,1)S(1)}, bf16[48,6144]{1,0:T(8,128)(2,1)S(1)}, u32[]{:S(2)}, u32[]{:S(2)}) %collective-permute-start.2) | collective-permute-done | bytes 589856 | tf_op jit(solution)/shard_map/ppermute | solution.py:271
  33.4 1.3 collective-permute-start.3
  34.7 4.6 %collective-permute-start.18 = (bf16[48,6144]{1,0:T(8,128)(2,1)S(1)}, bf16[48,6144]{1,0:T(8,128)(2,1)S(1)}, u32[]{:S(2)}, u32[]{:S(2)}) collective-permute-start(bf16[48,6144]{1,0:T(8,128)(2,1)S(1)} %get-tuple-element.109.own_ref), channel_id=1, source_target_pairs={{0,1},{1,2},{2,3},{4,5},{5,6},{6,7},{8,9},{9,10},{10,11},{12,13},{... | collective-permute-start | bytes 1769480 | tf_op jit(solution)/shard_map/ppermute | solution.py:272
  39.4 20.3 %collective-permute-start.38 = (bf16[48,6144]{1,0:T(8,128)(2,1)S(1)}, bf16[48,6144]{1,0:T(8,128)(2,1)S(1)}, u32[]{:S(2)}, u32[]{:S(2)}) collective-permute-start(bf16[48,6144]{1,0:T(8,128)(2,1)S(1)} %get-tuple-element.107.own_ref), channel_id=1, source_target_pairs={{0,2},{1,3},{2,0},{3,1},{4,6},{5,7},{6,4},{7,5},{8,10},{9,11},{10,... | collective-permute-start | bytes 1769480 | tf_op jit(solution)/shard_map/ppermute | solution.py:271
  59.7 1.3 collective-permute-start.19
  61.0 22.3 %collective-permute-done.20.far_ref = bf16[48,6144]{1,0:T(8,128)(2,1)} collective-permute-done((bf16[48,6144]{1,0:T(8,128)(2,1)S(1)}, bf16[48,6144]{1,0:T(8,128)(2,1)}, u32[]{:S(2)}, u32[]{:S(2)}) %collective-permute-start.20) | collective-permute-done | bytes 589856 | tf_op jit(solution)/shard_map/ppermute | solution.py:271
  83.3 1.3 collective-permute-start.21
  84.6 12.1 %shard_map.74 = (bf16[4,6144,256]{2,1,0:T(8,128)(2,1)S(1)}, bf16[4,6144,256]{2,1,0:T(8,128)(2,1)S(1)}, bf16[4,6144,256]{2,1,0:T(8,128)(2,1)S(1)}) custom-call(bf16[6144,1024]{1,0:T(8,128)(2,1)} %refs_0_.1, bf16[6144,1024]{1,0:T(8,128)(2,1)} %refs_1_.1, bf16[6144,1024]{1,0:T(8,128)(2,1)} %refs_2_.1), custom_call_target="tpu_custom_call" | custom-call | bytes 37748736 | tf_op jit(solution)/shard_map/pallas_call | solution.py:82
  96.7 4.6 %copy-done = bf16[4,6144,256]{2,1,0:T(8,128)(2,1)} copy-done((bf16[4,6144,256]{2,1,0:T(8,128)(2,1)}, bf16[4,6144,256]{2,1,0:T(8,128)(2,1)S(1)}, u32[]{:S(2)}) %copy-start) | copy-done | bytes 12582936
  101.3 6.2 %collective-permute-start.36 = (bf16[48,6144]{1,0:T(8,128)(2,1)S(1)}, bf16[48,6144]{1,0:T(8,128)(2,1)}, u32[]{:S(2)}, u32[]{:S(2)}) collective-permute-start(bf16[48,6144]{1,0:T(8,128)(2,1)S(1)} %get-tuple-element.107.own_ref), channel_id=1, source_target_pairs={{0,1},{1,2},{2,3},{4,5},{5,6},{6,7},{8,9},{9,10},{10,11},{12,13},{... | collective-permute-start | bytes 1769480 | tf_op jit(solution)/shard_map/ppermute | solution.py:272
  107.5 3.1 %shard_map.73.x_ref = bf16[192,6144]{1,0:T(8,128)(2,1)S(1)} custom-call(s32[3]{0:T(128)S(1)} %bitcast.11, bf16[48,6144]{1,0:T(8,128)(2,1)S(1)} %get-tuple-element.108.own_ref, bf16[48,6144]{1,0:T(8,128)(2,1)S(1)} %collective-permute-done.below_ref, bf16[48,6144]{1,0:T(8,128)(2,1)S(1)} %collective-permute-done.1.above_ref, ...), custom_call_target="tpu_custom_call" | custom-call | flops 11796480 | bytes 4718592 | tf_op jit(solution)/shard_map/pallas_call | solution.py:124
  110.7 0.8 copy-done.9
  111.5 1.3 collective-permute-start.37
  112.8 1.3 collective-permute-start.39
  114.1 4.6 %copy-done.1 = bf16[4,6144,256]{2,1,0:T(8,128)(2,1)S(1)} copy-done((bf16[4,6144,256]{2,1,0:T(8,128)(2,1)S(1)}, bf16[4,6144,256]{2,1,0:T(8,128)(2,1)}, u32[]{:S(2)}) %copy-start.1) | copy-done | bytes 12582936
  118.7 2.7 %shard_map.75 = (bf16[192,384]{1,0:T(8,128)(2,1)S(1)}, bf16[192,384]{1,0:T(8,128)(2,1)}) custom-call(bf16[192,6144]{1,0:T(8,128)(2,1)S(1)} %shard_map.73.x_ref, bf16[4,6144,256]{2,1,0:T(8,128)(2,1)S(1)} %get-tuple-element.56.wq_ref, bf16[4,6144,256]{2,1,0:T(8,128)(2,1)S(1)} %copy-done.1, bf16[4,6144,256]{2,1,0:T(8,128)(2,1)S(1)} %get-tuple-element.58.wv_ref), custom_call_target="tpu_custom_call" | custom-call | flops 1811939328 | bytes 294912 | tf_op jit(solution)/shard_map/pallas_call | solution.py:156
  121.3 4.6 %copy-done.3 = bf16[4,6144,256]{2,1,0:T(8,128)(2,1)} copy-done((bf16[4,6144,256]{2,1,0:T(8,128)(2,1)}, bf16[4,6144,256]{2,1,0:T(8,128)(2,1)S(1)}, u32[]{:S(2)}) %copy-start.3) | copy-done | bytes 12582936
  126.6 4.6 %copy-done.4 = bf16[4,6144,256]{2,1,0:T(8,128)(2,1)S(1)} copy-done((bf16[4,6144,256]{2,1,0:T(8,128)(2,1)S(1)}, bf16[4,6144,256]{2,1,0:T(8,128)(2,1)}, u32[]{:S(2)}) %copy-start.4) | copy-done | bytes 12582936
  131.2 4.3 %shard_map.76 = (bf16[192,384]{1,0:T(8,128)(2,1)}, bf16[192,384]{1,0:T(8,128)(2,1)S(1)}, bf16[192,384]{1,0:T(8,128)(2,1)S(1)}, bf16[192,384]{1,0:T(8,128)(2,1)S(1)}) custom-call(bf16[192,6144]{1,0:T(8,128)(2,1)S(1)} %shard_map.73.x_ref, bf16[4,6144,256]{2,1,0:T(8,128)(2,1)S(1)} %get-tuple-element.56.wq_ref, bf16[4,6144,256]{2,1,0:T(8,128)(2,1)S(1)} %copy-done.1, ...), custom_call_target="tpu_custom_call" | custom-call | flops 3623878656 | bytes 589824 | tf_op jit(solution)/shard_map/pallas_call | solution.py:156
  137.4 1.9 collective-permute-start.5
  139.3 1.1 copy-done.10
  140.4 5.0 %shard_map.79.x_ref = bf16[192,6144]{1,0:T(8,128)(2,1)S(1)} custom-call(s32[3]{0:T(128)S(1)} %bitcast.12, bf16[48,6144]{1,0:T(8,128)(2,1)S(1)} %get-tuple-element.109.own_ref, bf16[48,6144]{1,0:T(8,128)(2,1)S(1)} %copy-done.10, bf16[48,6144]{1,0:T(8,128)(2,1)} %collective-permute-done.19.above_ref, bf16[48,6144]{1,0:T(8,128)(2,1)} %collective-permute-done.20.far_ref, ...), custom_call_target="tpu_custom_call" | custom-call | flops 11796480 | bytes 4718592 | tf_op jit(solution)/shard_map/pallas_call | solution.py:124
  145.4 1.4 copy-done.7
  146.8 2.0 shard_map.77
  149.0 1.8 collective-permute-start.7
  151.5 2.6 %collective-permute-start.9 = (bf16[192,384]{1,0:T(8,128)(2,1)S(1)}, bf16[192,384]{1,0:T(8,128)(2,1)S(1)}, u32[]{:S(2)}, u32[]{:S(2)}) collective-permute-start(bf16[192,384]{1,0:T(8,128)(2,1)S(1)} %get-tuple-element.65), channel_id=1, source_target_pairs={{0,24},{4,28},{8,16},{12,20},{16,8},{20,12},{24,0},{28,4},{1,25},{... | collective-permute-start | bytes 442376 | tf_op jit(solution)/shard_map/ppermute | solution.py:256
  154.1 4.6 %copy-done.5 = bf16[4,6144,256]{2,1,0:T(8,128)(2,1)S(1)} copy-done((bf16[4,6144,256]{2,1,0:T(8,128)(2,1)S(1)}, bf16[4,6144,256]{2,1,0:T(8,128)(2,1)}, u32[]{:S(2)}) %copy-start.5) | copy-done | bytes 12582936
  158.7 1.7 copy-done.8
  160.4 7.5 %shard_map.80 = (bf16[192,384]{1,0:T(8,128)(2,1)S(1)}, bf16[192,384]{1,0:T(8,128)(2,1)S(1)}, bf16[192,384]{1,0:T(8,128)(2,1)S(1)}, bf16[192,384]{1,0:T(8,128)(2,...) custom-call(bf16[192,6144]{1,0:T(8,128)(2,1)S(1)} %copy-done.8, ...), custom_call_target="tpu_custom_call" | custom-call | flops 7247757312 | bytes 1179648 | tf_op jit(solution)/shard_map/pallas_call | solution.py:156
  167.8 4.8 %shard_map.82.x_ref = bf16[192,6144]{1,0:T(8,128)(2,1)S(1)} custom-call(s32[3]{0:T(128)S(1)} %bitcast.13, bf16[48,6144]{1,0:T(8,128)(2,1)S(1)} %get-tuple-element.107.own_ref, bf16[48,6144]{1,0:T(8,128)(2,1)} %collective-permute-done.36.below_ref, bf16[48,6144]{1,0:T(8,128)(2,1)} %collective-permute-done.37.above_ref, ...), custom_call_target="tpu_custom_call" | custom-call | flops 11796480 | bytes 4718592 | tf_op jit(solution)/shard_map/pallas_call | solution.py:124
  173.1 1.6 collective-permute-start.23
  174.7 1.6 collective-permute-start.25
  176.6 4.6 %copy-done.2 = bf16[4,6144,256]{2,1,0:T(8,128)(2,1)S(1)} copy-done((bf16[4,6144,256]{2,1,0:T(8,128)(2,1)S(1)}, bf16[4,6144,256]{2,1,0:T(8,128)(2,1)}, u32[]{:S(2)}) %copy-start.2) | copy-done | bytes 12582936
  181.2 7.5 %shard_map.83 = (bf16[192,384]{1,0:T(8,128)(2,1)S(1)}, bf16[192,384]{1,0:T(8,128)(2,1)S(1)}, bf16[192,384]{1,0:T(8,128)(2,1)S(1)}, bf16[192,384]{1,0:T(8,128)(2,...) custom-call(bf16[192,6144]{1,0:T(8,128)(2,1)S(1)} %shard_map.82.x_re, ...), custom_call_target="tpu_custom_call" | custom-call | flops 7247757312 | bytes 1179648 | tf_op jit(solution)/shard_map/pallas_call | solution.py:156
  188.7 2.7 %collective-permute-start.27 = (bf16[192,384]{1,0:T(8,128)(2,1)S(1)}, bf16[192,384]{1,0:T(8,128)(2,1)S(1)}, u32[]{:S(2)}, u32[]{:S(2)}) collective-permute-start(bf16[192,384]{1,0:T(8,128)(2,1)S(1)} %get-tuple-element.81), channel_id=1, source_target_pairs={{0,24},{4,28},{8,16},{12,20},{16,8},{20,12},{24,0},{28,4},{1,25},{... | collective-permute-start | bytes 442376 | tf_op jit(solution)/shard_map/ppermute | solution.py:256
  191.8 1.6 collective-permute-start.41
  193.4 2.8 %collective-permute-done.27.refs_6_ = bf16[192,384]{1,0:T(8,128)(2,1)S(1)} collective-permute-done((bf16[192,384]{1,0:T(8,128)(2,1)S(1)}, bf16[192,384]{1,0:T(8,128)(2,1)S(1)}, u32[]{:S(2)}, u32[]{:S(2)}) %collective-permute-start.27) | collective-permute-done | bytes 147488 | tf_op jit(solution)/shard_map/ppermute | solution.py:256
  196.2 1.8 collective-permute-start.43
  198.7 1.9 collective-permute-start.44
  200.6 1.4 collective-permute-start.45
  202.0 0.8 collective-permute-done.41.refs_2_
  202.9 4.6 %shard_map.78 = (bf16[192,128]{1,0:T(8,128)(2,1)S(1)}, bf16[192,128]{1,0:T(8,128)(2,1)S(1)}, bf16[192,128]{1,0:T(8,128)(2,1)S(1)}, bf16[192,128]{1,0:T(8,128)(2,...) custom-call(s32[8,8]{1,0:T(8,128)S(1)} %copy-done.22, ...), custom_call_target="tpu_custom_call" | custom-call | flops 679477248 | bytes 1572864 | tf_op jit(solution)/shard_map/pallas_call | solution.py:203
  207.5 1.6 collective-permute-start.11
  209.1 4.5 %shard_map.81 = (bf16[192,128]{1,0:T(8,128)(2,1)S(1)}, bf16[192,128]{1,0:T(8,128)(2,1)S(1)}, bf16[192,128]{1,0:T(8,128)(2,1)S(1)}, bf16[192,128]{1,0:T(8,128)(2,...) custom-call(s32[8,8]{1,0:T(8,128)S(1)} %copy-done.22, ...), custom_call_target="tpu_custom_call" | custom-call | flops 679477248 | bytes 1572864 | tf_op jit(solution)/shard_map/pallas_call | solution.py:203
  214.4 1.4 collective-permute-start.30
  216.3 1.3 collective-permute-start.32
  217.6 4.3 %shard_map.84 = (bf16[192,128]{1,0:T(8,128)(2,1)S(1)}, bf16[192,128]{1,0:T(8,128)(2,1)S(1)}, bf16[192,128]{1,0:T(8,128)(2,1)S(1)}, bf16[192,128]{1,0:T(8,128)(2,...) custom-call(s32[8,8]{1,0:T(8,128)S(1)} %copy-done.22, ...), custom_call_target="tpu_custom_call" | custom-call | flops 679477248 | bytes 1572864 | tf_op jit(solution)/shard_map/pallas_call | solution.py:203
  222.4 2.3 collective-permute-start.34
  225.4 1.3 collective-permute-start.48
  227.3 1.3 collective-permute-start.50
  229.8 1.3 collective-permute-start.52
  231.2 0.9 collective-permute-start.53
  232.1 1.5 collective-permute-start.13
  233.6 0.8 collective-permute-start.14
  234.8 1.8 collective-permute-start.16
  236.7 1.4 collective-permute-start.17
  238.0 0.9 shard_map.85.refs_8_
  238.9 0.9 shard_map.86.refs_8_
  241.1 0.9 shard_map.87
  (120 shorter events, 11.6 us)
Async XLA Ops:
  1.6 31.9 %collective-permute-start.2 = (bf16[48,6144]{1,0:T(8,128)(2,1)S(1)}, bf16[48,6144]{1,0:T(8,128)(2,1)S(1)}, u32[]{:S(2)}, u32[]{:S(2)}) collective-permute-start(bf16[48,6144]{1,0:T(8,128)(2,1)S(1)} %get-tuple-element.108.own_ref), channel_id=1, source_target_pairs={{0,2},{1,3},{2,0},{3,1},{4,6},{5,7},{6,4},{7,5},{8,10},{9,11},{10,... | collective-permute-start | bytes 1769480 | tf_op jit(solution)/shard_map/ppermute | solution.py:271
  5.7 33.7 %collective-permute-start = (bf16[48,6144]{1,0:T(8,128)(2,1)S(1)}, bf16[48,6144]{1,0:T(8,128)(2,1)S(1)}, u32[]{:S(2)}, u32[]{:S(2)}) collective-permute-start(bf16[48,6144]{1,0:T(8,128)(2,1)S(1)} %get-tuple-element.108.own_ref), channel_id=1, source_target_pairs={{0,1},{1,2},{2,3},{4,5},{5,6},{6,7},{8,9},{9,10},{10,11},{12,13},{... | collective-permute-start | bytes 1769480 | tf_op jit(solution)/shard_map/ppermute | solution.py:272
  9.2 50.5 %collective-permute-start.1 = (bf16[48,6144]{1,0:T(8,128)(2,1)S(1)}, bf16[48,6144]{1,0:T(8,128)(2,1)S(1)}, u32[]{:S(2)}, u32[]{:S(2)}) collective-permute-start(bf16[48,6144]{1,0:T(8,128)(2,1)S(1)} %get-tuple-element.108.own_ref), channel_id=1, source_target_pairs={{1,0},{2,1},{3,2},{5,4},{6,5},{7,6},{9,8},{10,9},{11,10},{13,12},{... | collective-permute-start | bytes 1769480 | tf_op jit(solution)/shard_map/ppermute | solution.py:273
  10.5 72.8 %collective-permute-start.20 = (bf16[48,6144]{1,0:T(8,128)(2,1)S(1)}, bf16[48,6144]{1,0:T(8,128)(2,1)}, u32[]{:S(2)}, u32[]{:S(2)}) collective-permute-start(bf16[48,6144]{1,0:T(8,128)(2,1)S(1)} %get-tuple-element.109.own_ref), channel_id=1, source_target_pairs={{0,2},{1,3},{2,0},{3,1},{4,6},{5,7},{6,4},{7,5},{8,10},{9,11},{10,... | collective-permute-start | bytes 1769480 | tf_op jit(solution)/shard_map/ppermute | solution.py:271
  33.4 67.9 %collective-permute-start.3 = (bf16[48,6144]{1,0:T(8,128)(2,1)S(1)}, bf16[48,6144]{1,0:T(8,128)(2,1)S(1)}, u32[]{:S(2)}, u32[]{:S(2)}) collective-permute-start(bf16[48,6144]{1,0:T(8,128)(2,1)S(1)} %collective-permute-done.2.far_ref), channel_id=1, source_target_pairs={{2,3},{1,0},{6,7},{5,4},{10,11},{9,8},{14,15},{13,12},{18,19},{17,... | collective-permute-start | bytes 1769480 | tf_op jit(solution)/shard_map/ppermute | solution.py:274
  34.7 75.9 %collective-permute-start.18 = (bf16[48,6144]{1,0:T(8,128)(2,1)S(1)}, bf16[48,6144]{1,0:T(8,128)(2,1)S(1)}, u32[]{:S(2)}, u32[]{:S(2)}) collective-permute-start(bf16[48,6144]{1,0:T(8,128)(2,1)S(1)} %get-tuple-element.109.own_ref), channel_id=1, source_target_pairs={{0,1},{1,2},{2,3},{4,5},{5,6},{6,7},{8,9},{9,10},{10,11},{12,13},{... | collective-permute-start | bytes 1769480 | tf_op jit(solution)/shard_map/ppermute | solution.py:272
  39.4 68.2 %copy-start.6 = (bf16[50,2,6144]{2,1,0:T(2,128)(2,1)S(1)}, bf16[50,2,6144]{2,1,0:T(2,128)(2,1)}, u32[]{:S(2)}) copy-start(bf16[50,2,6144]{2,1,0:T(2,128)(2,1)} %mod_ref.5) | copy-start | bytes 3686404
  39.4 68.1 %copy-start.11 = (s32[1,3]{1,0:T(1,128)S(1)}, s32[1,3]{1,0:T(1,128)}, u32[]{:S(2)}) copy-start(s32[1,3]{1,0:T(1,128)} %param.8) | copy-start | bytes 40
  39.4 73.4 %collective-permute-start.38 = (bf16[48,6144]{1,0:T(8,128)(2,1)S(1)}, bf16[48,6144]{1,0:T(8,128)(2,1)S(1)}, u32[]{:S(2)}, u32[]{:S(2)}) collective-permute-start(bf16[48,6144]{1,0:T(8,128)(2,1)S(1)} %get-tuple-element.107.own_ref), channel_id=1, source_target_pairs={{0,2},{1,3},{2,0},{3,1},{4,6},{5,7},{6,4},{7,5},{8,10},{9,11},{10,... | collective-permute-start | bytes 1769480 | tf_op jit(solution)/shard_map/ppermute | solution.py:271
  59.7 77.7 %collective-permute-start.19 = (bf16[48,6144]{1,0:T(8,128)(2,1)S(1)}, bf16[48,6144]{1,0:T(8,128)(2,1)}, u32[]{:S(2)}, u32[]{:S(2)}) collective-permute-start(bf16[48,6144]{1,0:T(8,128)(2,1)S(1)} %get-tuple-element.109.own_ref), channel_id=1, source_target_pairs={{1,0},{2,1},{3,2},{5,4},{6,5},{7,6},{9,8},{10,9},{11,10},{13,12},{... | collective-permute-start | bytes 1769480 | tf_op jit(solution)/shard_map/ppermute | solution.py:273
  83.3 54.1 %collective-permute-start.21 = (bf16[48,6144]{1,0:T(8,128)(2,1)}, bf16[48,6144]{1,0:T(8,128)(2,1)}, u32[]{:S(2)}, u32[]{:S(2)}) collective-permute-start(bf16[48,6144]{1,0:T(8,128)(2,1)} %collective-permute-done.20.far_ref), channel_id=1, source_target_pairs={{2,3},{1,0},{6,7},{5,4},{10,11},{9,8},{14,15},{13,12},{18,19},{17,... | collective-permute-start | bytes 1769480 | tf_op jit(solution)/shard_map/ppermute | solution.py:274
  101.3 47.5 %collective-permute-start.36 = (bf16[48,6144]{1,0:T(8,128)(2,1)S(1)}, bf16[48,6144]{1,0:T(8,128)(2,1)}, u32[]{:S(2)}, u32[]{:S(2)}) collective-permute-start(bf16[48,6144]{1,0:T(8,128)(2,1)S(1)} %get-tuple-element.107.own_ref), channel_id=1, source_target_pairs={{0,1},{1,2},{2,3},{4,5},{5,6},{6,7},{8,9},{9,10},{10,11},{12,13},{... | collective-permute-start | bytes 1769480 | tf_op jit(solution)/shard_map/ppermute | solution.py:272
  111.5 37.5 %collective-permute-start.37 = (bf16[48,6144]{1,0:T(8,128)(2,1)S(1)}, bf16[48,6144]{1,0:T(8,128)(2,1)}, u32[]{:S(2)}, u32[]{:S(2)}) collective-permute-start(bf16[48,6144]{1,0:T(8,128)(2,1)S(1)} %get-tuple-element.107.own_ref), channel_id=1, source_target_pairs={{1,0},{2,1},{3,2},{5,4},{6,5},{7,6},{9,8},{10,9},{11,10},{13,12},{... | collective-permute-start | bytes 1769480 | tf_op jit(solution)/shard_map/ppermute | solution.py:273
  112.8 38.0 %collective-permute-start.39 = (bf16[48,6144]{1,0:T(8,128)(2,1)S(1)}, bf16[48,6144]{1,0:T(8,128)(2,1)}, u32[]{:S(2)}, u32[]{:S(2)}) collective-permute-start(bf16[48,6144]{1,0:T(8,128)(2,1)S(1)} %collective-permute-done.38.far_ref), channel_id=1, source_target_pairs={{2,3},{1,0},{6,7},{5,4},{10,11},{9,8},{14,15},{13,12},{18,19},{17,... | collective-permute-start | bytes 1769480 | tf_op jit(solution)/shard_map/ppermute | solution.py:274
  118.7 28.1 %slice-start = ((s8[12582912]{0:T(1024)(128)(4,1)}), s8[4194304]{0:T(1024)(128)(4,1)S(1)}, s32[]{:S(2)}) async-start(s8[12582912]{0:T(1024)(128)(4,1)} %bitcast.7), calls=%async_computation | async-start | bytes 8388608
  118.7 28.1 %slice-start.1 = ((s8[12582912]{0:T(1024)(128)(4,1)}), s8[4194304]{0:T(1024)(128)(4,1)S(1)}, s32[]{:S(2)}) async-start(s8[12582912]{0:T(1024)(128)(4,1)} %bitcast.7), calls=%async_computation.1 | async-start | bytes 8388608
  131.2 15.6 %slice-start.2 = ((s8[12582912]{0:T(1024)(128)(4,1)}), s8[4194304]{0:T(1024)(128)(4,1)S(1)}, s32[]{:S(2)}) async-start(s8[12582912]{0:T(1024)(128)(4,1)} %bitcast.7), calls=%async_computation.2 | async-start | bytes 8388608
  137.4 13.4 %collective-permute-start.4 = (bf16[192,384]{1,0:T(8,128)(2,1)}, bf16[192,384]{1,0:T(8,128)(2,1)S(1)}, u32[]{:S(2)}, u32[]{:S(2)}) collective-permute-start(bf16[192,384]{1,0:T(8,128)(2,1)} %get-tuple-element.60), channel_id=1, source_target_pairs={{0,4},{4,0},{8,12},{12,8},{16,20},{20,16},{24,28},{28,24},{1,5},{5... | collective-permute-start | bytes 442376 | tf_op jit(solution)/shard_map/ppermute | solution.py:256
  137.4 16.6 %collective-permute-start.5 = (bf16[192,384]{1,0:T(8,128)(2,1)}, bf16[192,384]{1,0:T(8,128)(2,1)}, u32[]{:S(2)}, u32[]{:S(2)}) collective-permute-start(bf16[192,384]{1,0:T(8,128)(2,1)} %get-tuple-element.61), channel_id=1, source_target_pairs={{0,8},{4,12},{8,0},{12,4},{16,24},{20,28},{24,16},{28,20},{1,9},{5... | collective-permute-start | bytes 442376 | tf_op jit(solution)/shard_map/ppermute | solution.py:256
  140.4 13.7 %slice-start.3 = ((s8[12582912]{0:T(1024)(128)(4,1)}), s8[4194304]{0:T(1024)(128)(4,1)S(1)}, s32[]{:S(2)}) async-start(s8[12582912]{0:T(1024)(128)(4,1)} %bitcast.9), calls=%async_computation.3 | async-start | bytes 8388608
  146.8 7.3 %slice-start.4 = ((s8[12582912]{0:T(1024)(128)(4,1)}), s8[4194304]{0:T(1024)(128)(4,1)S(1)}, s32[]{:S(2)}) async-start(s8[12582912]{0:T(1024)(128)(4,1)} %bitcast.9), calls=%async_computation.4 | async-start | bytes 8388608
  148.9 23.7 %collective-permute-start.6 = (bf16[192,384]{1,0:T(8,128)(2,1)S(1)}, bf16[192,384]{1,0:T(8,128)(2,1)S(1)}, u32[]{:S(2)}, u32[]{:S(2)}) collective-permute-start(bf16[192,384]{1,0:T(8,128)(2,1)S(1)} %copy-done.21), channel_id=1, source_target_pairs={{0,12},{4,8},{8,4},{12,0},{16,28},{20,24},{24,20},{28,16},{1,13},{... | collective-permute-start | bytes 442376 | tf_op jit(solution)/shard_map/ppermute | solution.py:256
  149.0 24.1 %collective-permute-start.7 = (bf16[192,384]{1,0:T(8,128)(2,1)S(1)}, bf16[192,384]{1,0:T(8,128)(2,1)S(1)}, u32[]{:S(2)}, u32[]{:S(2)}) collective-permute-start(bf16[192,384]{1,0:T(8,128)(2,1)S(1)} %copy-done.19), channel_id=1, source_target_pairs={{0,16},{4,20},{8,24},{12,28},{16,0},{20,4},{24,8},{28,12},{1,17},{... | collective-permute-start | bytes 442376 | tf_op jit(solution)/shard_map/ppermute | solution.py:256
  150.8 24.0 %collective-permute-start.8 = (bf16[192,384]{1,0:T(8,128)(2,1)S(1)}, bf16[192,384]{1,0:T(8,128)(2,1)S(1)}, u32[]{:S(2)}, u32[]{:S(2)}) collective-permute-start(bf16[192,384]{1,0:T(8,128)(2,1)S(1)} %copy-done.17), channel_id=1, source_target_pairs={{0,20},{4,16},{8,28},{12,24},{16,4},{20,0},{24,12},{28,8},{1,21},{... | collective-permute-start | bytes 442376 | tf_op jit(solution)/shard_map/ppermute | solution.py:256
  151.5 23.3 %collective-permute-start.9 = (bf16[192,384]{1,0:T(8,128)(2,1)S(1)}, bf16[192,384]{1,0:T(8,128)(2,1)S(1)}, u32[]{:S(2)}, u32[]{:S(2)}) collective-permute-start(bf16[192,384]{1,0:T(8,128)(2,1)S(1)} %get-tuple-element.65), channel_id=1, source_target_pairs={{0,24},{4,28},{8,16},{12,20},{16,8},{20,12},{24,0},{28,4},{1,25},{... | collective-permute-start | bytes 442376 | tf_op jit(solution)/shard_map/ppermute | solution.py:256
  154.0 22.3 %collective-permute-start.10 = (bf16[192,384]{1,0:T(8,128)(2,1)S(1)}, bf16[192,384]{1,0:T(8,128)(2,1)S(1)}, u32[]{:S(2)}, u32[]{:S(2)}) collective-permute-start(bf16[192,384]{1,0:T(8,128)(2,1)S(1)} %get-tuple-element.66), channel_id=1, source_target_pairs={{0,28},{4,24},{8,20},{12,16},{16,12},{20,8},{24,4},{28,0},{1,29},{... | collective-permute-start | bytes 442376 | tf_op jit(solution)/shard_map/ppermute | solution.py:256
  172.6 16.0 %collective-permute-start.22 = (bf16[192,384]{1,0:T(8,128)(2,1)S(1)}, bf16[192,384]{1,0:T(8,128)(2,1)S(1)}, u32[]{:S(2)}, u32[]{:S(2)}) collective-permute-start(bf16[192,384]{1,0:T(8,128)(2,1)S(1)} %get-tuple-element.76), channel_id=1, source_target_pairs={{0,4},{4,0},{8,12},{12,8},{16,20},{20,16},{24,28},{28,24},{1,5},{5... | collective-permute-start | bytes 442376 | tf_op jit(solution)/shard_map/ppermute | solution.py:256
  173.1 18.2 %collective-permute-start.23 = (bf16[192,384]{1,0:T(8,128)(2,1)S(1)}, bf16[192,384]{1,0:T(8,128)(2,1)S(1)}, u32[]{:S(2)}, u32[]{:S(2)}) collective-permute-start(bf16[192,384]{1,0:T(8,128)(2,1)S(1)} %get-tuple-element.77), channel_id=1, source_target_pairs={{0,8},{4,12},{8,0},{12,4},{16,24},{20,28},{24,16},{28,20},{1,9},{5... | collective-permute-start | bytes 442376 | tf_op jit(solution)/shard_map/ppermute | solution.py:256
  174.7 16.6 %collective-permute-start.24 = (bf16[192,384]{1,0:T(8,128)(2,1)S(1)}, bf16[192,384]{1,0:T(8,128)(2,1)S(1)}, u32[]{:S(2)}, u32[]{:S(2)}) collective-permute-start(bf16[192,384]{1,0:T(8,128)(2,1)S(1)} %get-tuple-element.78), channel_id=1, source_target_pairs={{0,12},{4,8},{8,4},{12,0},{16,28},{20,24},{24,20},{28,16},{1,13},{... | collective-permute-start | bytes 442376 | tf_op jit(solution)/shard_map/ppermute | solution.py:256
  174.7 17.0 %collective-permute-start.25 = (bf16[192,384]{1,0:T(8,128)(2,1)S(1)}, bf16[192,384]{1,0:T(8,128)(2,1)S(1)}, u32[]{:S(2)}, u32[]{:S(2)}) collective-permute-start(bf16[192,384]{1,0:T(8,128)(2,1)S(1)} %get-tuple-element.79), channel_id=1, source_target_pairs={{0,16},{4,20},{8,24},{12,28},{16,0},{20,4},{24,8},{28,12},{1,17},{... | collective-permute-start | bytes 442376 | tf_op jit(solution)/shard_map/ppermute | solution.py:256
  176.3 17.1 %collective-permute-start.26 = (bf16[192,384]{1,0:T(8,128)(2,1)S(1)}, bf16[192,384]{1,0:T(8,128)(2,1)S(1)}, u32[]{:S(2)}, u32[]{:S(2)}) collective-permute-start(bf16[192,384]{1,0:T(8,128)(2,1)S(1)} %get-tuple-element.80), channel_id=1, source_target_pairs={{0,20},{4,16},{8,28},{12,24},{16,4},{20,0},{24,12},{28,8},{1,21},{... | collective-permute-start | bytes 442376 | tf_op jit(solution)/shard_map/ppermute | solution.py:256
  181.2 21.7 %copy-start.13 = (bf16[192,384]{1,0:T(8,128)(2,1)S(1)}, bf16[192,384]{1,0:T(8,128)(2,1)}, u32[]{:S(2)}) copy-start(bf16[192,384]{1,0:T(8,128)(2,1)} %copy-done.12) | copy-start | bytes 442372
  181.2 21.7 %copy-start.15 = (bf16[192,384]{1,0:T(8,128)(2,1)S(1)}, bf16[192,384]{1,0:T(8,128)(2,1)}, u32[]{:S(2)}) copy-start(bf16[192,384]{1,0:T(8,128)(2,1)} %copy-done.14) | copy-start | bytes 442372
  181.2 21.7 %copy-start.22 = (s32[8,8]{1,0:T(8,128)S(1)}, s32[8,8]{1,0:T(8,128)}, u32[]{:S(2)}) copy-start(s32[8,8]{1,0:T(8,128)} %mask_ref.5) | copy-start | bytes 772
  188.7 7.6 %collective-permute-start.27 = (bf16[192,384]{1,0:T(8,128)(2,1)S(1)}, bf16[192,384]{1,0:T(8,128)(2,1)S(1)}, u32[]{:S(2)}, u32[]{:S(2)}) collective-permute-start(bf16[192,384]{1,0:T(8,128)(2,1)S(1)} %get-tuple-element.81), channel_id=1, source_target_pairs={{0,24},{4,28},{8,16},{12,20},{16,8},{20,12},{24,0},{28,4},{1,25},{... | collective-permute-start | bytes 442376 | tf_op jit(solution)/shard_map/ppermute | solution.py:256
  191.3 7.4 %collective-permute-start.28 = (bf16[192,384]{1,0:T(8,128)(2,1)S(1)}, bf16[192,384]{1,0:T(8,128)(2,1)S(1)}, u32[]{:S(2)}, u32[]{:S(2)}) collective-permute-start(bf16[192,384]{1,0:T(8,128)(2,1)S(1)} %get-tuple-element.82), channel_id=1, source_target_pairs={{0,28},{4,24},{8,20},{12,16},{16,12},{20,8},{24,4},{28,0},{1,29},{... | collective-permute-start | bytes 442376 | tf_op jit(solution)/shard_map/ppermute | solution.py:256
  191.3 9.3 %collective-permute-start.40 = (bf16[192,384]{1,0:T(8,128)(2,1)S(1)}, bf16[192,384]{1,0:T(8,128)(2,1)S(1)}, u32[]{:S(2)}, u32[]{:S(2)}) collective-permute-start(bf16[192,384]{1,0:T(8,128)(2,1)S(1)} %get-tuple-element.92), channel_id=1, source_target_pairs={{0,4},{4,0},{8,12},{12,8},{16,20},{20,16},{24,28},{28,24},{1,5},{5... | collective-permute-start | bytes 442376 | tf_op jit(solution)/shard_map/ppermute | solution.py:256
  191.8 11.1 %collective-permute-start.41 = (bf16[192,384]{1,0:T(8,128)(2,1)S(1)}, bf16[192,384]{1,0:T(8,128)(2,1)S(1)}, u32[]{:S(2)}, u32[]{:S(2)}) collective-permute-start(bf16[192,384]{1,0:T(8,128)(2,1)S(1)} %get-tuple-element.93), channel_id=1, source_target_pairs={{0,8},{4,12},{8,0},{12,4},{16,24},{20,28},{24,16},{28,20},{1,9},{5... | collective-permute-start | bytes 442376 | tf_op jit(solution)/shard_map/ppermute | solution.py:256
  193.4 14.1 %collective-permute-start.42 = (bf16[192,384]{1,0:T(8,128)(2,1)S(1)}, bf16[192,384]{1,0:T(8,128)(2,1)S(1)}, u32[]{:S(2)}, u32[]{:S(2)}) collective-permute-start(bf16[192,384]{1,0:T(8,128)(2,1)S(1)} %get-tuple-element.94), channel_id=1, source_target_pairs={{0,12},{4,8},{8,4},{12,0},{16,28},{20,24},{24,20},{28,16},{1,13},{... | collective-permute-start | bytes 442376 | tf_op jit(solution)/shard_map/ppermute | solution.py:256
  196.2 17.4 %collective-permute-start.43 = (bf16[192,384]{1,0:T(8,128)(2,1)S(1)}, bf16[192,384]{1,0:T(8,128)(2,1)S(1)}, u32[]{:S(2)}, u32[]{:S(2)}) collective-permute-start(bf16[192,384]{1,0:T(8,128)(2,1)S(1)} %get-tuple-element.95), channel_id=1, source_target_pairs={{0,16},{4,20},{8,24},{12,28},{16,0},{20,4},{24,8},{28,12},{1,17},{... | collective-permute-start | bytes 442376 | tf_op jit(solution)/shard_map/ppermute | solution.py:256
  198.7 15.7 %collective-permute-start.44 = (bf16[192,384]{1,0:T(8,128)(2,1)S(1)}, bf16[192,384]{1,0:T(8,128)(2,1)S(1)}, u32[]{:S(2)}, u32[]{:S(2)}) collective-permute-start(bf16[192,384]{1,0:T(8,128)(2,1)S(1)} %get-tuple-element.96), channel_id=1, source_target_pairs={{0,20},{4,16},{8,28},{12,24},{16,4},{20,0},{24,12},{28,8},{1,21},{... | collective-permute-start | bytes 442376 | tf_op jit(solution)/shard_map/ppermute | solution.py:256
  200.6 13.8 %collective-permute-start.45 = (bf16[192,384]{1,0:T(8,128)(2,1)S(1)}, bf16[192,384]{1,0:T(8,128)(2,1)S(1)}, u32[]{:S(2)}, u32[]{:S(2)}) collective-permute-start(bf16[192,384]{1,0:T(8,128)(2,1)S(1)} %get-tuple-element.97), channel_id=1, source_target_pairs={{0,24},{4,28},{8,16},{12,20},{16,8},{20,12},{24,0},{28,4},{1,25},{... | collective-permute-start | bytes 442376 | tf_op jit(solution)/shard_map/ppermute | solution.py:256
  202.9 13.0 %collective-permute-start.46 = (bf16[192,384]{1,0:T(8,128)(2,1)S(1)}, bf16[192,384]{1,0:T(8,128)(2,1)S(1)}, u32[]{:S(2)}, u32[]{:S(2)}) collective-permute-start(bf16[192,384]{1,0:T(8,128)(2,1)S(1)} %get-tuple-element.98), channel_id=1, source_target_pairs={{0,28},{4,24},{8,20},{12,16},{16,12},{20,8},{24,4},{28,0},{1,29},{... | collective-permute-start | bytes 442376 | tf_op jit(solution)/shard_map/ppermute | solution.py:256
  207.5 8.8 %collective-permute-start.11 = (bf16[192,128]{1,0:T(8,128)(2,1)S(1)}, bf16[192,128]{1,0:T(8,128)(2,1)S(1)}, u32[]{:S(2)}, u32[]{:S(2)}) collective-permute-start(bf16[192,128]{1,0:T(8,128)(2,1)S(1)} %get-tuple-element.68), channel_id=1, source_target_pairs={{0,4},{4,0},{8,12},{12,8},{16,20},{20,16},{24,28},{28,24},{1,5},{5... | collective-permute-start | bytes 147464 | tf_op jit(solution)/shard_map/ppermute | solution.py:256
  213.6 8.3 %collective-permute-start.12 = (bf16[192,128]{1,0:T(8,128)(2,1)S(1)}, bf16[192,128]{1,0:T(8,128)(2,1)S(1)}, u32[]{:S(2)}, u32[]{:S(2)}) collective-permute-start(bf16[192,128]{1,0:T(8,128)(2,1)S(1)} %get-tuple-element.69), channel_id=1, source_target_pairs={{0,8},{4,12},{8,0},{12,4},{16,24},{20,28},{24,16},{28,20},{1,9},{5... | collective-permute-start | bytes 147464 | tf_op jit(solution)/shard_map/ppermute | solution.py:256
  214.4 7.9 %collective-permute-start.29 = (bf16[192,128]{1,0:T(8,128)(2,1)S(1)}, bf16[192,128]{1,0:T(8,128)(2,1)S(1)}, u32[]{:S(2)}, u32[]{:S(2)}) collective-permute-start(bf16[192,128]{1,0:T(8,128)(2,1)S(1)} %get-tuple-element.84), channel_id=1, source_target_pairs={{0,4},{4,0},{8,12},{12,8},{16,20},{20,16},{24,28},{28,24},{1,5},{5... | collective-permute-start | bytes 147464 | tf_op jit(solution)/shard_map/ppermute | solution.py:256
  214.4 10.2 %collective-permute-start.30 = (bf16[192,128]{1,0:T(8,128)(2,1)S(1)}, bf16[192,128]{1,0:T(8,128)(2,1)S(1)}, u32[]{:S(2)}, u32[]{:S(2)}) collective-permute-start(bf16[192,128]{1,0:T(8,128)(2,1)S(1)} %get-tuple-element.85), channel_id=1, source_target_pairs={{0,8},{4,12},{8,0},{12,4},{16,24},{20,28},{24,16},{28,20},{1,9},{5... | collective-permute-start | bytes 147464 | tf_op jit(solution)/shard_map/ppermute | solution.py:256
  215.8 9.2 %collective-permute-start.31 = (bf16[192,128]{1,0:T(8,128)(2,1)S(1)}, bf16[192,128]{1,0:T(8,128)(2,1)S(1)}, u32[]{:S(2)}, u32[]{:S(2)}) collective-permute-start(bf16[192,128]{1,0:T(8,128)(2,1)S(1)} %get-tuple-element.86), channel_id=1, source_target_pairs={{0,12},{4,8},{8,4},{12,0},{16,28},{20,24},{24,20},{28,16},{1,13},{... | collective-permute-start | bytes 147464 | tf_op jit(solution)/shard_map/ppermute | solution.py:256
  216.3 9.1 %collective-permute-start.32 = (bf16[192,128]{1,0:T(8,128)(2,1)S(1)}, bf16[192,128]{1,0:T(8,128)(2,1)S(1)}, u32[]{:S(2)}, u32[]{:S(2)}) collective-permute-start(bf16[192,128]{1,0:T(8,128)(2,1)S(1)} %get-tuple-element.87), channel_id=1, source_target_pairs={{0,16},{4,20},{8,24},{12,28},{16,0},{20,4},{24,8},{28,12},{1,17},{... | collective-permute-start | bytes 147464 | tf_op jit(solution)/shard_map/ppermute | solution.py:256
  221.9 4.8 %collective-permute-start.33 = (bf16[192,128]{1,0:T(8,128)(2,1)S(1)}, bf16[192,128]{1,0:T(8,128)(2,1)S(1)}, u32[]{:S(2)}, u32[]{:S(2)}) collective-permute-start(bf16[192,128]{1,0:T(8,128)(2,1)S(1)} %get-tuple-element.88), channel_id=1, source_target_pairs={{0,20},{4,16},{8,28},{12,24},{16,4},{20,0},{24,12},{28,8},{1,21},{... | collective-permute-start | bytes 147464 | tf_op jit(solution)/shard_map/ppermute | solution.py:256
  222.4 5.0 %collective-permute-start.34 = (bf16[192,128]{1,0:T(8,128)(2,1)S(1)}, bf16[192,128]{1,0:T(8,128)(2,1)S(1)}, u32[]{:S(2)}, u32[]{:S(2)}) collective-permute-start(bf16[192,128]{1,0:T(8,128)(2,1)S(1)} %get-tuple-element.89), channel_id=1, source_target_pairs={{0,24},{4,28},{8,16},{12,20},{16,8},{20,12},{24,0},{28,4},{1,25},{... | collective-permute-start | bytes 147464 | tf_op jit(solution)/shard_map/ppermute | solution.py:256
  224.6 4.6 %collective-permute-start.35 = (bf16[192,128]{1,0:T(8,128)(2,1)S(1)}, bf16[192,128]{1,0:T(8,128)(2,1)S(1)}, u32[]{:S(2)}, u32[]{:S(2)}) collective-permute-start(bf16[192,128]{1,0:T(8,128)(2,1)S(1)} %get-tuple-element.90), channel_id=1, source_target_pairs={{0,28},{4,24},{8,20},{12,16},{16,12},{20,8},{24,4},{28,0},{1,29},{... | collective-permute-start | bytes 147464 | tf_op jit(solution)/shard_map/ppermute | solution.py:256
  225.0 4.8 %collective-permute-start.47 = (bf16[192,128]{1,0:T(8,128)(2,1)S(1)}, bf16[192,128]{1,0:T(8,128)(2,1)S(1)}, u32[]{:S(2)}, u32[]{:S(2)}) collective-permute-start(bf16[192,128]{1,0:T(8,128)(2,1)S(1)} %get-tuple-element.100), channel_id=1, source_target_pairs={{0,4},{4,0},{8,12},{12,8},{16,20},{20,16},{24,28},{28,24},{1,5},{5... | collective-permute-start | bytes 147464 | tf_op jit(solution)/shard_map/ppermute | solution.py:256
  225.4 5.8 %collective-permute-start.48 = (bf16[192,128]{1,0:T(8,128)(2,1)S(1)}, bf16[192,128]{1,0:T(8,128)(2,1)S(1)}, u32[]{:S(2)}, u32[]{:S(2)}) collective-permute-start(bf16[192,128]{1,0:T(8,128)(2,1)S(1)} %get-tuple-element.101), channel_id=1, source_target_pairs={{0,8},{4,12},{8,0},{12,4},{16,24},{20,28},{24,16},{28,20},{1,9},{5... | collective-permute-start | bytes 147464 | tf_op jit(solution)/shard_map/ppermute | solution.py:256
  226.7 5.4 %collective-permute-start.49 = (bf16[192,128]{1,0:T(8,128)(2,1)S(1)}, bf16[192,128]{1,0:T(8,128)(2,1)S(1)}, u32[]{:S(2)}, u32[]{:S(2)}) collective-permute-start(bf16[192,128]{1,0:T(8,128)(2,1)S(1)} %get-tuple-element.102), channel_id=1, source_target_pairs={{0,12},{4,8},{8,4},{12,0},{16,28},{20,24},{24,20},{28,16},{1,13},{... | collective-permute-start | bytes 147464 | tf_op jit(solution)/shard_map/ppermute | solution.py:256
  227.3 6.3 %collective-permute-start.50 = (bf16[192,128]{1,0:T(8,128)(2,1)S(1)}, bf16[192,128]{1,0:T(8,128)(2,1)S(1)}, u32[]{:S(2)}, u32[]{:S(2)}) collective-permute-start(bf16[192,128]{1,0:T(8,128)(2,1)S(1)} %get-tuple-element.103), channel_id=1, source_target_pairs={{0,16},{4,20},{8,24},{12,28},{16,0},{20,4},{24,8},{28,12},{1,17},{... | collective-permute-start | bytes 147464 | tf_op jit(solution)/shard_map/ppermute | solution.py:256
  229.2 5.2 %collective-permute-start.51 = (bf16[192,128]{1,0:T(8,128)(2,1)S(1)}, bf16[192,128]{1,0:T(8,128)(2,1)S(1)}, u32[]{:S(2)}, u32[]{:S(2)}) collective-permute-start(bf16[192,128]{1,0:T(8,128)(2,1)S(1)} %get-tuple-element.104), channel_id=1, source_target_pairs={{0,20},{4,16},{8,28},{12,24},{16,4},{20,0},{24,12},{28,8},{1,21},{... | collective-permute-start | bytes 147464 | tf_op jit(solution)/shard_map/ppermute | solution.py:256
  229.8 5.0 %collective-permute-start.52 = (bf16[192,128]{1,0:T(8,128)(2,1)S(1)}, bf16[192,128]{1,0:T(8,128)(2,1)S(1)}, u32[]{:S(2)}, u32[]{:S(2)}) collective-permute-start(bf16[192,128]{1,0:T(8,128)(2,1)S(1)} %get-tuple-element.105), channel_id=1, source_target_pairs={{0,24},{4,28},{8,16},{12,20},{16,8},{20,12},{24,0},{28,4},{1,25},{... | collective-permute-start | bytes 147464 | tf_op jit(solution)/shard_map/ppermute | solution.py:256
  231.2 5.5 %collective-permute-start.53 = (bf16[192,128]{1,0:T(8,128)(2,1)S(1)}, bf16[192,128]{1,0:T(8,128)(2,1)S(1)}, u32[]{:S(2)}, u32[]{:S(2)}) collective-permute-start(bf16[192,128]{1,0:T(8,128)(2,1)S(1)} %get-tuple-element.106), channel_id=1, source_target_pairs={{0,28},{4,24},{8,20},{12,16},{16,12},{20,8},{24,4},{28,0},{1,29},{... | collective-permute-start | bytes 147464 | tf_op jit(solution)/shard_map/ppermute | solution.py:256
  232.1 7.6 %collective-permute-start.13 = (bf16[192,128]{1,0:T(8,128)(2,1)S(1)}, bf16[192,128]{1,0:T(8,128)(2,1)S(1)}, u32[]{:S(2)}, u32[]{:S(2)}) collective-permute-start(bf16[192,128]{1,0:T(8,128)(2,1)S(1)} %get-tuple-element.70), channel_id=1, source_target_pairs={{0,12},{4,8},{8,4},{12,0},{16,28},{20,24},{24,20},{28,16},{1,13},{... | collective-permute-start | bytes 147464 | tf_op jit(solution)/shard_map/ppermute | solution.py:256
  233.6 6.1 %collective-permute-start.14 = (bf16[192,128]{1,0:T(8,128)(2,1)S(1)}, bf16[192,128]{1,0:T(8,128)(2,1)S(1)}, u32[]{:S(2)}, u32[]{:S(2)}) collective-permute-start(bf16[192,128]{1,0:T(8,128)(2,1)S(1)} %get-tuple-element.71), channel_id=1, source_target_pairs={{0,16},{4,20},{8,24},{12,28},{16,0},{20,4},{24,8},{28,12},{1,17},{... | collective-permute-start | bytes 147464 | tf_op jit(solution)/shard_map/ppermute | solution.py:256
  234.4 5.3 %collective-permute-start.15 = (bf16[192,128]{1,0:T(8,128)(2,1)S(1)}, bf16[192,128]{1,0:T(8,128)(2,1)S(1)}, u32[]{:S(2)}, u32[]{:S(2)}) collective-permute-start(bf16[192,128]{1,0:T(8,128)(2,1)S(1)} %get-tuple-element.72), channel_id=1, source_target_pairs={{0,20},{4,16},{8,28},{12,24},{16,4},{20,0},{24,12},{28,8},{1,21},{... | collective-permute-start | bytes 147464 | tf_op jit(solution)/shard_map/ppermute | solution.py:256
  234.8 5.5 %collective-permute-start.16 = (bf16[192,128]{1,0:T(8,128)(2,1)S(1)}, bf16[192,128]{1,0:T(8,128)(2,1)S(1)}, u32[]{:S(2)}, u32[]{:S(2)}) collective-permute-start(bf16[192,128]{1,0:T(8,128)(2,1)S(1)} %get-tuple-element.73), channel_id=1, source_target_pairs={{0,24},{4,28},{8,16},{12,20},{16,8},{20,12},{24,0},{28,4},{1,25},{... | collective-permute-start | bytes 147464 | tf_op jit(solution)/shard_map/ppermute | solution.py:256
  236.7 4.4 %collective-permute-start.17 = (bf16[192,128]{1,0:T(8,128)(2,1)S(1)}, bf16[192,128]{1,0:T(8,128)(2,1)S(1)}, u32[]{:S(2)}, u32[]{:S(2)}) collective-permute-start(bf16[192,128]{1,0:T(8,128)(2,1)S(1)} %get-tuple-element.74), channel_id=1, source_target_pairs={{0,28},{4,24},{8,20},{12,16},{16,12},{20,8},{24,4},{28,0},{1,29},{... | collective-permute-start | bytes 147464 | tf_op jit(solution)/shard_map/ppermute | solution.py:256
  (19 other events, 51.3 us)
